TPU v7x, 128 devices: a whole 4x4x4 slice. The times are simulated.
128 devices in a mesh: pts: 32 (over z, x, core), rep: 4 (over y).
Axes of the slice: x: 4, y: 4, z: 4, core: 2. Of those that a mesh axis runs over, the one named last changes fastest.
Arguments:
- target_xyz: float32 [3, 32768], P(None, 'pts'), may hold values from 0 to 1
- source_xyz: float32 [3, 65536], P(None, ('pts', 'rep')), may hold values from 0 to 1
- target_count: int32 [32], P('pts'), may hold values from 1 to 1024, as said below
- source_count: int32 [128], P(('pts', 'rep')), may hold values from 1 to 512, as said below
- psi: bfloat16 [32768, 256], P('pts'), may hold values from -6 to 6
- omega: bfloat16 [65536, 256], P(('pts', 'rep')), may hold values from -6 to 6
Outputs:
- range_sketch: float32 [32768, 256], P('pts')
- corange_sketch: float32 [65536, 256], P(('pts', 'rep'))
- core: float32 [256, 256], replicated
- range_gram: float32 [256, 256], replicated
- corange_gram: float32 [256, 256], replicated
Inputs may be any that keep to these rules, and one draw needn't show every extreme that they name: `target_count`: each group holds 1 to 1024 live targets; some group holds exactly 1024. `source_count`: each shard holds 1 to 512 live sources; some shard holds exactly 512.
All inputs are finite; a program needn't handle non-finite values.
Results may differ from a plain program's by a relative error of at most 0.0003.
The roundings to bfloat16 on the way count: a program that leaves them out, or rounds other values in their place, can miss the bound.
Values may be sent and summed in bfloat16 or wider, within the bound.
No kernel may reach another device: no remote copies, remote signals or barrier semaphores. Data moves between devices by JAX's collectives and lax.ppermute only.
A program may use at most 64 MiB of HBM per device.

v0:
```python
import math
import jax
import jax.numpy as jnp
from jax import lax
from jax.sharding import PartitionSpec as P

SHIFT = 1.05
SPREAD = 8.0


def tile_block(tgt, src):
    dx = tgt[0][:, None] - (src[0][None, :] + SHIFT)
    dy = SPREAD * (tgt[1][:, None] - src[1][None, :])
    dz = SPREAD * (tgt[2][:, None] - src[2][None, :])
    return lax.rsqrt(dx * dx + dy * dy + dz * dz).astype(jnp.bfloat16)


def local(target_xyz, source_xyz, target_count, source_count, psi, omega):
    tcap = psi.shape[0]
    scap = omega.shape[0]
    width = psi.shape[1]
    n_pts = lax.axis_size("pts")
    n_rep = lax.axis_size("rep")
    all_targets = tcap * n_pts
    all_sources = scap * n_pts * n_rep
    tlive = jnp.arange(tcap, dtype=jnp.int32) < target_count[0]
    slive = jnp.arange(scap, dtype=jnp.int32) < source_count[0]
    psi_live = jnp.where(tlive[:, None], psi, jnp.zeros_like(psi))
    omega_live = jnp.where(slive[:, None], omega, jnp.zeros_like(omega))
    hi = lax.Precision.HIGHEST
    src_all = lax.all_gather(source_xyz, "pts", axis=1, tiled=True)
    piece = lax.all_gather(omega_live, "pts", axis=0, tiled=True)

    def range_inner(j, acc):
        rows = lax.dynamic_slice_in_dim(piece, j * scap, scap, 0)
        where = lax.dynamic_slice_in_dim(src_all, j * scap, scap, 1)
        return acc + jnp.dot(
            tile_block(target_xyz, where), rows, preferred_element_type=jnp.float32
        )

    y_part = lax.fori_loop(
        0, piece.shape[0] // scap, range_inner, jnp.zeros((tcap, width), jnp.float32)
    )
    y_sum = lax.psum(y_part, "rep") * (2.0 / math.sqrt(all_sources))
    range_sketch = jnp.where(tlive[:, None], y_sum, jnp.zeros_like(y_sum))
    tgt_all = lax.all_gather(target_xyz, "pts", axis=1, tiled=True)
    corange_piece = lax.all_gather(psi_live, "pts", axis=0, tiled=True)

    def corange_inner(j, acc):
        rows = lax.dynamic_slice_in_dim(corange_piece, j * tcap, tcap, 0)
        where = lax.dynamic_slice_in_dim(tgt_all, j * tcap, tcap, 1)
        tile = tile_block(where, source_xyz)
        return acc + lax.dot_general(
            tile, rows, (((0,), (0,)), ((), ())), preferred_element_type=jnp.float32
        )

    z_sum = lax.fori_loop(
        0, corange_piece.shape[0] // tcap, corange_inner, jnp.zeros((scap, width), jnp.float32)
    )
    z_scaled = z_sum * (2.0 / math.sqrt(all_targets))
    corange_sketch = jnp.where(slive[:, None], z_scaled, jnp.zeros_like(z_scaled))
    z_gram_part = jnp.dot(corange_sketch.T, corange_sketch, precision=hi)
    core_part = jnp.dot(psi_live.astype(jnp.float32).T, range_sketch, precision=hi)
    y_gram_part = jnp.dot(range_sketch.T, range_sketch, precision=hi)
    core_sum, y_gram = lax.psum((core_part, y_gram_part), "pts")
    z_gram = lax.psum(z_gram_part, ("pts", "rep"))
    core = core_sum / math.sqrt(all_targets)
    range_gram = y_gram / all_targets
    corange_gram = z_gram / all_sources
    return (range_sketch, corange_sketch, core, range_gram, corange_gram)


def solution(mesh):
    return jax.shard_map(
        local,
        mesh=mesh,
        in_specs=(
            P(None, "pts"),
            P(None, ("pts", "rep")),
            P("pts"),
            P(("pts", "rep")),
            P("pts", None),
            P(("pts", "rep"), None),
        ),
        out_specs=(P("pts", None), P(("pts", "rep"), None), P(), P(), P()),
        check_vma=False,
    )
```

profile of v0, /device:TPU:1, one launch (start us, length us, event | category | flops | bytes accessed | tf_op | source)
XLA Modules:
  0.0 550.0 jit_solution(14603858195827019406)
XLA Ops:
  9.7 27.6 %all_gather.12 = f32[3,16384]{1,0:T(4,128)S(1)} all-gather(f32[3,512]{1,0:T(4,128)} %param.11), channel_id=1, replica_groups=mesh['pts'=32,'rep'=4] {'pts'}, dimensions={1}, use_global_device_ids=true | all-gather | bytes 202752 | tf_op jit(solution)/shard_map/all_gather | solution.py:31
  37.3 30.2 %all-gather.3.cloned.1.call-done = bf16[16384,256]{1,0:T(8,128)(2,1)} async-done(((bf16[512,256]{1,0:T(8,128)(2,1)}), bf16[16384,256]{1,0:T(8,128)(2,1)}) %all-gather.3.cloned.1.call-update) | async-done | bytes 8388624 | tf_op jit(solution)/shard_map/all_gather | solution.py:32
  67.5 96.4 %while.28 = (s32[]{:T(128)}, f32[1024,256]{1,0:T(8,128)S(1)}, f32[3,1024]{1,0:T(4,128)}, f32[3,16384]{1,0:T(4,128)S(1)}, bf16[16384,256]{1,0:T(8,128)(2,1)}, /*i...) while((s32[]{:T(128)}, f32[1024,256]{1,0:T(8,128)S(1)}, ...), condition=%wide.region_1.2_spmd.clone, body=%wide.region_0.1_spmd.clone.sunk | while | flops 274727424 | bytes 2414797 | solution.py:41
  166.7 24.7 %all_gather.14 = f32[3,32768]{1,0:T(4,128)S(1)} all-gather(f32[3,1024]{1,0:T(4,128)S(1)} %copy-done.5), channel_id=1, replica_groups=mesh['pts'=32,'rep'=4] {'pts'}, dimensions={1}, use_global_device_ids=true | all-gather | bytes 405504 | tf_op jit(solution)/shard_map/all_gather | solution.py:46
  191.4 17.0 %all-reduce.5.cloned.1.call-done = f32[1024,256]{1,0:T(8,128)} async-done(((f32[1024,256]{1,0:T(8,128)}), f32[1024,256]{1,0:T(8,128)}) %all-reduce.5.cloned.1.call-update) | async-done | bytes 1048592 | tf_op jit(solution)/shard_map/psum | solution.py:44
  211.4 2.6 fusion.22
  214.0 73.1 %all-gather.5.cloned.1.call-done = bf16[32768,256]{1,0:T(8,128)(2,1)} async-done(((bf16[1024,256]{1,0:T(8,128)(2,1)}), bf16[32768,256]{1,0:T(8,128)(2,1)}) %all-gather.5.cloned.1.call-update) | async-done | bytes 16777232 | tf_op jit(solution)/shard_map/all_gather | solution.py:47
  287.1 81.4 %while.29 = (s32[]{:T(128)}, f32[512,256]{1,0:T(8,128)S(1)}, f32[3,32768]{1,0:T(4,128)S(1)}, f32[3,512]{1,0:T(4,128)S(1)}, bf16[32768,256]{1,0:T(8,128)(2,1)}, /...) while((s32[]{:T(128)}, f32[512,256]{1,0:T(8,128)S(1)}, ...), condition=%wide.region_4.5_spmd.clone, body=%wide.region_3.4_spmd.clone.sunk | while | flops 274465280 | bytes 1628365 | solution.py:57
  287.2 2.4 convolution_add_fusion.5
  292.3 2.4 convolution_add_fusion.5
  297.4 2.4 convolution_add_fusion.5
  300.0 2.4 convolution_add_fusion.5
  305.0 2.4 convolution_add_fusion.5
  315.2 2.4 convolution_add_fusion.5
  317.8 2.4 convolution_add_fusion.5
  320.3 2.4 convolution_add_fusion.5
  322.9 2.4 convolution_add_fusion.5
  327.9 2.4 convolution_add_fusion.5
  333.0 2.4 convolution_add_fusion.5
  338.1 2.4 convolution_add_fusion.5
  348.3 2.4 convolution_add_fusion.5
  350.9 2.4 convolution_add_fusion.5
  370.5 24.1 %all-reduce.9.cloned.1.call-done = (f32[256,256]{1,0:T(8,128)}, f32[256,256]{1,0:T(8,128)}) async-done(((f32[256,256]{1,0:T(8,128)}, f32[256,256]{1,0:T(8,128)}), (f32[256,256]{1,0:T(8,128)}, f32[256,256]{1,0:T(8,128)})) %all-reduce.9.cloned.1.call-update) | async-done | bytes 524304 | tf_op jit(solution)/shard_map/psum | solution.py:65
  396.4 145.4 %all-reduce.7.cloned.1.call-done = f32[256,256]{1,0:T(8,128)} async-done(((f32[256,256]{1,0:T(8,128)}), f32[256,256]{1,0:T(8,128)}) %all-reduce.7.cloned.1.call-update) | async-done | bytes 262160 | tf_op jit(solution)/shard_map/psum | solution.py:66
  (214 shorter events, 154.1 us)
Async XLA Ops:
  7.2 60.3 %all-gather.3.cloned.1.call-start = ((), (), s32[]{:S(2)}) async-start(), calls=%async_computation | async-start | bytes 8650752 | tf_op jit(solution)/shard_map/all_gather | solution.py:32
  9.7 198.7 %all-reduce.5.cloned.1.call-start = ((), (), s32[]{:S(2)}) async-start(), calls=%async_computation.1 | async-start | bytes 2097152 | tf_op jit(solution)/shard_map/psum | solution.py:44
  67.5 98.1 %copy-start.4 = (bf16[1024,256]{1,0:T(8,128)(2,1)S(1)}, bf16[1024,256]{1,0:T(8,128)(2,1)}, u32[]{:S(2)}) copy-start(bf16[1024,256]{1,0:T(8,128)(2,1)} %param.14) | copy-start | bytes 1572868
  163.9 1.0 copy-start.3
  163.9 2.8 copy-start.5
  164.9 122.2 %all-gather.5.cloned.1.call-start = ((), (), s32[]{:S(2)}) async-start(), calls=%async_computation.2 | async-start | bytes 17301504 | tf_op jit(solution)/shard_map/all_gather | solution.py:47
  166.6 43.2 %copy-start.2 = (bf16[1024,256]{1,0:T(8,128)(2,1)S(1)}, bf16[1024,256]{1,0:T(8,128)(2,1)}, u32[]{:S(2)}) copy-start(bf16[1024,256]{1,0:T(8,128)(2,1)} %broadcast_select_fusion) | copy-start | bytes 1572868
  166.6 227.9 %all-reduce.9.cloned.1.call-start = ((), (), s32[]{:S(2)}) async-start(), calls=%async_computation.4 | async-start | bytes 1048576 | tf_op jit(solution)/shard_map/psum | solution.py:65
  209.8 4.1 copy-start
  209.9 77.3 %copy-start.6 = (f32[3,512]{1,0:T(4,128)S(1)}, f32[3,512]{1,0:T(4,128)}, u32[]{:S(2)}) copy-start(f32[3,512]{1,0:T(4,128)} %param.11) | copy-start | bytes 18436
  214.0 327.8 %all-reduce.7.cloned.1.call-start = ((), (), s32[]{:S(2)}) async-start(), calls=%async_computation.3 | async-start | bytes 524288 | tf_op jit(solution)/shard_map/psum | solution.py:66
  368.7 174.8 %copy-start.1 = (f32[512,256]{1,0:T(8,128)}, f32[512,256]{1,0:T(8,128)S(1)}, u32[]{:S(2)}) copy-start(f32[512,256]{1,0:T(8,128)S(1)} %multiply_select_fusion.1) | copy-start | bytes 1572868
Sparse Core Ops, SparseCore 0:
  10.8 56.6 all-gather.2
  165.0 43.3 all-reduce.4
  211.2 75.8 all-gather.4
  290.8 103.6 all-reduce.8
  399.1 142.5 all-reduce.6
where the time goes:
time: 555 us; the launch traced here: 550 us
  waiting for transfers between devices  290 us (52%)
  matrix products  148 us (27%)
  blocking collectives  52.2 us (9%)
  local copies, waits for them, and re-layouts  30.9 us (6%)
  between operations  15.2 us (3%)
  other arithmetic  10.8 us (2%)
    psum x1, waiting for transfers between devices, local(): z_gram = lax.psum(z_gram_part, ('pts', 'rep'))  145 us
    dot_general x32, matrix products, corange_inner(): lax.dot_general(tile, rows, (((0,), (0,)), ((), ())), preferred_element_t...  76.9 us
    all_gather x1, waiting for transfers between devices, local(): corange_piece = lax.all_gather(psi_live, 'pts', axis=0, tiled=True)  73.1 us
    dot_general x32, matrix products, range_inner(): jnp.dot(tile_block(target_xyz, where), rows, preferred_element_type=jnp.f...  65.5 us
    all_gather x1, waiting for transfers between devices, local(): piece = lax.all_gather(omega_live, 'pts', axis=0, tiled=True)  30.2 us
    slice x64, local copies, waits for them, and re-layouts, tile_block(): dx = tgt[0][:, None] - (src[0][None, :] + SHIFT)  30 us
    all_gather x1, blocking collectives, local(): src_all = lax.all_gather(source_xyz, 'pts', axis=1, tiled=True)  27.6 us
    all_gather x1, blocking collectives, local(): tgt_all = lax.all_gather(target_xyz, 'pts', axis=1, tiled=True)  24.7 us
  transfers between devices with their start and end apart: 5, of which 5 were waited for; matrix products, arithmetic and copies ran while one was open for 16% of the time, Pallas kernels for 0%

commit v1 on v0

--- a/solution.py
+++ b/solution.py
@@ -63,7 +63,7 @@
     core_part = jnp.dot(psi_live.astype(jnp.float32).T, range_sketch, precision=hi)
     y_gram_part = jnp.dot(range_sketch.T, range_sketch, precision=hi)
     core_sum, y_gram = lax.psum((core_part, y_gram_part), "pts")
-    z_gram = lax.psum(z_gram_part, ("pts", "rep"))
+    z_gram = lax.psum(lax.psum(z_gram_part, "pts"), "rep")
     core = core_sum / math.sqrt(all_targets)
     range_gram = y_gram / all_targets
     corange_gram = z_gram / all_sources

time: 555 us -> 530 us (0.955)
  waiting for transfers between devices: 290 us -> 264 us
    psum x1, waiting for transfers between devices: 145 us -> 39.7 us  [local(): z_gram = lax.psum(lax.psum(z_gram_part, 'pts'), 'rep')]
    psum x1, waiting for transfers between devices: 24.1 us -> 104 us  [local(): core_sum, y_gram = lax.psum((core_part, y_gram_part), 'pts')]
  transfers between devices with their start and end apart: 5 -> 5, of which waited for: 5 -> 5; matrix products, arithmetic and copies ran while one was open for 16% -> 2% of each run, Pallas kernels for 0% -> 0%
where the time goes in v1:
time: 530 us; the launch traced here: 524 us
  waiting for transfers between devices  264 us (50%)
  matrix products  148 us (28%)
  blocking collectives  52.2 us (10%)
  local copies, waits for them, and re-layouts  30.9 us (6%)
  between operations  15.2 us (3%)
  other arithmetic  10.8 us (2%)
    psum x1, waiting for transfers between devices, local(): core_sum, y_gram = lax.psum((core_part, y_gram_part), 'pts')  104 us
    dot_general x32, matrix products, corange_inner(): lax.dot_general(tile, rows, (((0,), (0,)), ((), ())), preferred_element_t...  77 us
    all_gather x1, waiting for transfers between devices, local(): corange_piece = lax.all_gather(psi_live, 'pts', axis=0, tiled=True)  73.1 us
    dot_general x32, matrix products, range_inner(): jnp.dot(tile_block(target_xyz, where), rows, preferred_element_type=jnp.f...  65.5 us
    psum x1, waiting for transfers between devices, local(): z_gram = lax.psum(lax.psum(z_gram_part, 'pts'), 'rep')  39.7 us
    all_gather x1, waiting for transfers between devices, local(): piece = lax.all_gather(omega_live, 'pts', axis=0, tiled=True)  30.2 us
    slice x64, local copies, waits for them, and re-layouts, tile_block(): dx = tgt[0][:, None] - (src[0][None, :] + SHIFT)  29.9 us
    all_gather x1, blocking collectives, local(): src_all = lax.all_gather(source_xyz, 'pts', axis=1, tiled=True)  27.6 us
  transfers between devices with their start and end apart: 5, of which 5 were waited for; matrix products, arithmetic and copies ran while one was open for 2% of the time, Pallas kernels for 0%

profile of v1, /device:TPU:1, one launch (start us, length us, event | category | flops | bytes accessed | tf_op | source)
XLA Modules:
  0.0 523.9 jit_solution(3442788399810201816)
XLA Ops:
  9.7 27.6 %all_gather.12 = f32[3,16384]{1,0:T(4,128)S(1)} all-gather(f32[3,512]{1,0:T(4,128)} %param.11), channel_id=1, replica_groups=mesh['pts'=32,'rep'=4] {'pts'}, dimensions={1}, use_global_device_ids=true | all-gather | bytes 202752 | tf_op jit(solution)/shard_map/all_gather | solution.py:31
  37.3 30.2 %all-gather.3.cloned.1.call-done = bf16[16384,256]{1,0:T(8,128)(2,1)} async-done(((bf16[512,256]{1,0:T(8,128)(2,1)}), bf16[16384,256]{1,0:T(8,128)(2,1)}) %all-gather.3.cloned.1.call-update) | async-done | bytes 8388624 | tf_op jit(solution)/shard_map/all_gather | solution.py:32
  67.5 96.4 %while.28 = (s32[]{:T(128)}, f32[1024,256]{1,0:T(8,128)S(1)}, f32[3,1024]{1,0:T(4,128)}, f32[3,16384]{1,0:T(4,128)S(1)}, bf16[16384,256]{1,0:T(8,128)(2,1)}, /*i...) while((s32[]{:T(128)}, f32[1024,256]{1,0:T(8,128)S(1)}, ...), condition=%wide.region_1.2_spmd.clone, body=%wide.region_0.1_spmd.clone.sunk | while | flops 274727424 | bytes 2414797 | solution.py:41
  166.7 24.7 %all_gather.14 = f32[3,32768]{1,0:T(4,128)S(1)} all-gather(f32[3,1024]{1,0:T(4,128)S(1)} %copy-done.5), channel_id=1, replica_groups=mesh['pts'=32,'rep'=4] {'pts'}, dimensions={1}, use_global_device_ids=true | all-gather | bytes 405504 | tf_op jit(solution)/shard_map/all_gather | solution.py:46
  191.4 17.0 %all-reduce.5.cloned.1.call-done = f32[1024,256]{1,0:T(8,128)} async-done(((f32[1024,256]{1,0:T(8,128)}), f32[1024,256]{1,0:T(8,128)}) %all-reduce.5.cloned.1.call-update) | async-done | bytes 1048592 | tf_op jit(solution)/shard_map/psum | solution.py:44
  211.4 2.6 fusion.22
  214.0 73.1 %all-gather.5.cloned.1.call-done = bf16[32768,256]{1,0:T(8,128)(2,1)} async-done(((bf16[1024,256]{1,0:T(8,128)(2,1)}), bf16[32768,256]{1,0:T(8,128)(2,1)}) %all-gather.5.cloned.1.call-update) | async-done | bytes 16777232 | tf_op jit(solution)/shard_map/all_gather | solution.py:47
  287.1 81.4 %while.29 = (s32[]{:T(128)}, f32[512,256]{1,0:T(8,128)S(1)}, f32[3,32768]{1,0:T(4,128)S(1)}, f32[3,512]{1,0:T(4,128)S(1)}, bf16[32768,256]{1,0:T(8,128)(2,1)}, /...) while((s32[]{:T(128)}, f32[512,256]{1,0:T(8,128)S(1)}, ...), condition=%wide.region_4.5_spmd.clone, body=%wide.region_3.4_spmd.clone.sunk | while | flops 274465280 | bytes 1628365 | solution.py:57
  289.8 2.4 convolution_add_fusion.5
  294.8 2.4 convolution_add_fusion.5
  299.9 2.4 convolution_add_fusion.5
  305.0 2.4 convolution_add_fusion.5
  310.1 2.4 convolution_add_fusion.5
  315.2 2.4 convolution_add_fusion.5
  320.3 2.4 convolution_add_fusion.5
  325.4 2.4 convolution_add_fusion.5
  330.4 2.4 convolution_add_fusion.5
  335.5 2.4 convolution_add_fusion.5
  340.6 2.4 convolution_add_fusion.5
  345.7 2.4 convolution_add_fusion.5
  350.8 2.4 convolution_add_fusion.5
  355.9 2.4 convolution_add_fusion.5
  370.5 103.7 %all-reduce.9.cloned.1.call-done = (f32[256,256]{1,0:T(8,128)}, f32[256,256]{1,0:T(8,128)}, f32[256,256]{1,0:T(8,128)}) async-done(((f32[256,256]{1,0:T(8,128)}, f32[256,256]{1,0:T(8,128)}, f32[256,256]{1,0:T(8,128)}), (f32[256,256]{1,0:T(8,128)}, f32[256,256]{1,0:T(8,128)}, f32[256,256]{1,0:T(8,128)})) %all-reduce.9.cloned.1.call-update) | async-done | bytes 786448 | tf_op jit(solution)/shard_map/psum | solution.py:65
  476.0 39.7 %all-reduce.7.cloned.1.call-done = f32[256,256]{1,0:T(8,128)} async-done(((f32[256,256]{1,0:T(8,128)}), f32[256,256]{1,0:T(8,128)}) %all-reduce.7.cloned.1.call-update) | async-done | bytes 262160 | tf_op jit(solution)/shard_map/psum | solution.py:66
  (214 shorter events, 154.0 us)
Async XLA Ops:
  7.2 60.3 %all-gather.3.cloned.1.call-start = ((), (), s32[]{:S(2)}) async-start(), calls=%async_computation | async-start | bytes 8650752 | tf_op jit(solution)/shard_map/all_gather | solution.py:32
  9.7 198.7 %all-reduce.5.cloned.1.call-start = ((), (), s32[]{:S(2)}) async-start(), calls=%async_computation.1 | async-start | bytes 2097152 | tf_op jit(solution)/shard_map/psum | solution.py:44
  67.5 98.1 %copy-start.4 = (bf16[1024,256]{1,0:T(8,128)(2,1)S(1)}, bf16[1024,256]{1,0:T(8,128)(2,1)}, u32[]{:S(2)}) copy-start(bf16[1024,256]{1,0:T(8,128)(2,1)} %param.14) | copy-start | bytes 1572868
  163.9 1.0 copy-start.3
  163.9 2.8 copy-start.5
  164.9 122.2 %all-gather.5.cloned.1.call-start = ((), (), s32[]{:S(2)}) async-start(), calls=%async_computation.2 | async-start | bytes 17301504 | tf_op jit(solution)/shard_map/all_gather | solution.py:47
  166.6 43.2 %copy-start.2 = (bf16[1024,256]{1,0:T(8,128)(2,1)S(1)}, bf16[1024,256]{1,0:T(8,128)(2,1)}, u32[]{:S(2)}) copy-start(bf16[1024,256]{1,0:T(8,128)(2,1)} %broadcast_select_fusion) | copy-start | bytes 1572868
  166.6 307.5 %all-reduce.9.cloned.1.call-start = ((), (), s32[]{:S(2)}) async-start(), calls=%async_computation.4 | async-start | bytes 1572864 | tf_op jit(solution)/shard_map/psum | solution.py:65
  209.8 4.1 copy-start
  209.9 77.3 %copy-start.6 = (f32[3,512]{1,0:T(4,128)S(1)}, f32[3,512]{1,0:T(4,128)}, u32[]{:S(2)}) copy-start(f32[3,512]{1,0:T(4,128)} %param.11) | copy-start | bytes 18436
  368.6 148.8 %copy-start.1 = (f32[512,256]{1,0:T(8,128)}, f32[512,256]{1,0:T(8,128)S(1)}, u32[]{:S(2)}) copy-start(f32[512,256]{1,0:T(8,128)S(1)} %multiply_select_fusion.1) | copy-start | bytes 1572868
  370.4 145.3 %all-reduce.7.cloned.1.call-start = ((), (), s32[]{:S(2)}) async-start(), calls=%async_computation.3 | async-start | bytes 524288 | tf_op jit(solution)/shard_map/psum | solution.py:66
Sparse Core Ops, SparseCore 0:
  10.8 56.6 all-gather.2
  165.0 43.3 all-reduce.4
  211.2 75.8 all-gather.4
  370.5 103.5 all-reduce.8
  476.3 39.4 all-reduce.6
